TPU v7x, 32 devices: a whole 2x2x4 slice. The times are simulated.
32 devices in a mesh: region: 2 (over x), shard: 16 (over z, y, core).
Axes of the slice: x: 2, y: 2, z: 4, core: 2. Of those that a mesh axis runs over, the one named last changes fastest.
Arguments:
- queries: bfloat16 [48, 1024], replicated, may hold values from -6 to 6
- database: bfloat16 [16384, 1024], P(('region', 'shard')), may hold values from -6 to 6
- neighbour_ids: int32 [48, 10], replicated, may hold values from 0 to 16383
- tile_weights: bfloat16 [64, 13, 4, 256], P(('region', 'shard')), may hold values from 0.0019989014 to 0.059814453
- tile_columns: int32 [64, 13, 4, 256], P(('region', 'shard')), may hold values from 0 to 255
- tile_owner: int32 [64, 13], P(('region', 'shard')), may hold values from 0 to 15, all different within a row; in each aligned block of 2 rows (0 to 1, 2 to 3, ...) at most 2 rows name the same one
- tile_block: int32 [64, 13], P(('region', 'shard')), may hold values from 0 to 1
Outputs:
- diffused: float32 [48, 16384], P(None, ('region', 'shard'))
Inputs may be any that keep to these rules, and one draw needn't show every extreme that they name: `tile_owner`: each row names 13 different owners; among the rows of one device's blocks no owner is named more than 2 times, and that many in some devices.
All inputs are finite; a program needn't handle non-finite values.
Results may differ from a plain program's by a relative error of at most 0.005.
Values may be sent and summed in bfloat16 or wider, within the bound.
A program may use at most 64 MiB of HBM per device.

v0:
```python
import math
import jax
import jax.numpy as jnp
from jax import lax
from jax.sharding import PartitionSpec as P

EPS = 1e-06
BETA = 0.8


def unit_rows(matrix):
    return matrix / jnp.sqrt(jnp.sum(matrix * matrix, axis=1, keepdims=True) + EPS)


def per_device(
    queries, database, neighbour_ids, tile_weights, tile_columns, tile_owner, tile_block
):
    rows_dev = database.shape[0]
    feature_width = database.shape[1]
    unit_query = unit_rows(queries.astype(jnp.float32)).astype(jnp.bfloat16)
    first_row = lax.axis_index(("region", "shard")) * rows_dev
    similar = lax.dot_general(
        unit_query, database, (((1,), (1,)), ((), ())), preferred_element_type=jnp.float32
    )
    positive = jnp.maximum(similar, 0.0)
    weights = (positive * positive * positive / math.sqrt(feature_width)).astype(jnp.bfloat16)
    local_ids = neighbour_ids - first_row
    row_ids = lax.broadcasted_iota(jnp.int32, (1, 1, rows_dev), 2)
    counts = jnp.sum((local_ids[:, :, None] == row_ids).astype(jnp.float32), axis=1)
    chosen = (counts * weights.astype(jnp.float32)).astype(jnp.bfloat16)
    local_term = jnp.dot(chosen, database, preferred_element_type=jnp.float32)
    expanded_sum = lax.psum(local_term, ("region", "shard")) + unit_query.astype(jnp.float32)
    expanded = unit_rows(expanded_sum).astype(jnp.bfloat16)
    products = lax.dot_general(
        expanded, database, (((1,), (1,)), ((), ())), preferred_element_type=jnp.float32
    )
    scores = jnp.maximum(products, 0.0).astype(jnp.bfloat16)
    blocks_dev = tile_columns.shape[0]
    tile_count = tile_columns.shape[1]
    edge_count = tile_columns.shape[2]
    block_rows = tile_columns.shape[3]
    query_count = scores.shape[0]
    score_blocks = scores.reshape(query_count, blocks_dev, block_rows)
    owners = tile_owner.reshape(-1)
    block_ids = tile_block.reshape(-1)
    sources = owners * blocks_dev + block_ids

    def fetch_blocks(current):
        region_blocks = lax.all_gather(current, "shard", axis=1, tiled=True)
        return region_blocks.reshape(query_count, -1)

    column_base = (sources * block_rows).reshape(blocks_dev, tile_count, 1, 1)
    flat_columns = column_base + tile_columns

    def spread(current):
        flat = fetch_blocks(current)
        total = jnp.zeros((query_count, blocks_dev, block_rows), jnp.float32)
        for edge in range(edge_count):
            reached = jnp.take(flat, flat_columns[:, :, edge, :], axis=1)
            scaled = (
                reached.astype(jnp.float32) * tile_weights[:, :, edge, :].astype(jnp.float32)[None]
            )
            total = total + jnp.sum(scaled, axis=2)
        return total

    source = score_blocks.astype(jnp.float32)
    current = score_blocks
    current = (source + BETA * spread(current)).astype(jnp.bfloat16)
    diffused = source + BETA * spread(current)
    return diffused.reshape(query_count, blocks_dev * block_rows)


def solution(mesh):
    placed = (
        P(),
        P(("region", "shard"), None),
        P(),
        P(("region", "shard"), None, None, None),
        P(("region", "shard"), None, None, None),
        P(("region", "shard"), None),
        P(("region", "shard"), None),
    )
    return jax.shard_map(
        per_device,
        mesh=mesh,
        in_specs=placed,
        out_specs=P(None, ("region", "shard")),
        check_vma=False,
    )
```

profile of v0, /device:TPU:0, one launch (start us, length us, event | category | flops | bytes accessed | tf_op | source)
XLA Modules:
  0.0 358.0 jit_solution(2654204438736871811)
XLA Ops:
  6.6 0.8 broadcast_subtract_fusion
  7.4 0.2 convert_reduce_fusion
  7.5 1.0 fusion.1
  8.6 2.3 fusion.8
  11.0 0.1 broadcast_add_fusion
  11.1 0.1 fusion.21
  11.1 0.1 compare_and_fusion
  11.3 0.1 fusion.22
  11.5 0.6 pad_clamp_fusion.2
  12.1 0.6 copy.164
  12.7 0.6 pad_clamp_fusion.1
  13.3 0.6 copy.172
  13.9 0.6 copy.179
  14.5 0.6 fusion.14
  15.2 0.6 fusion.12
  15.8 0.6 pad_clamp_fusion
  16.4 123.9 %all-reduce.2.cloned.1.call-done = f32[48,1024]{1,0:T(8,128)} async-done(((f32[48,1024]{1,0:T(8,128)}), f32[48,1024]{1,0:T(8,128)}) %all-reduce.2.cloned.1.call-update) | async-done | bytes 196624 | tf_op jit(solution)/shard_map/psum | solution.py:32
  140.3 1.1 multiply_reduce_fusion.8
  141.4 1.4 fusion
  142.8 25.9 %all_gather.6 = bf16[48,32,256]{2,0,1:T(8,128)(2,1)} all-gather(bf16[48,2,256]{2,0,1:T(8,128)(2,1)S(1)} %bitcast.89), channel_id=1, replica_groups=mesh['region'=2,'shard'=16] {'shard'}, dimensions={1}, use_global_device_ids=true | all-gather | bytes 835584 | tf_op jit(solution)/shard_map/all_gather | solution.py:49
  168.7 2.0 copy.158
  170.7 14.2 %gather_fusion = bf16[6656,48]{1,0:T(8,128)(2,1)} fusion(bf16[48,8192]{0,1:T(8,128)(2,1)S(1)} %bitcast.70, s32[7168]{0:T(1024)S(1)} %pad_clamp_fusion.3), kind=kCustom, calls=%fused_computation.clone | custom fusion | bytes 1304576 | tf_op jit(solution)/shard_map/jit(_take)/gather | solution.py:59
  184.9 5.3 %multiply_reduce_fusion.7 = f32[48,2,256]{0,2,1:T(8,128)S(1)} fusion(bf16[2,13,256,48]{3,2,1,0:T(8,128)(2,1)} %bitcast.84, f32[2,13,256]{2,1,0:T(8,128)S(1)} %get-tuple-element.29, pred[2,13,256]{2,1,0:T(8,128)(4,1)S(1)} %copy.154), kind=kLoop, calls=%fused_computation.15 | loop fusion | flops 1253376 | bytes 770560 | tf_op jit(solution)/shard_map/reduce_sum | solution.py:63
  190.2 0.1 copy.169
  190.3 15.4 %gather_fusion.1 = bf16[6656,48]{1,0:T(8,128)(2,1)} fusion(bf16[48,8192]{0,1:T(8,128)(2,1)S(1)} %bitcast.71, s32[7168]{0:T(1024)} %pad_clamp_fusion.2), kind=kCustom, calls=%fused_computation.1.clone | custom fusion | bytes 1304576 | tf_op jit(solution)/shard_map/jit(_take)/gather | solution.py:59
  205.7 5.4 %multiply_reduce_fusion.6 = f32[48,2,256]{0,2,1:T(8,128)S(1)} fusion(bf16[2,13,256,48]{3,2,1,0:T(8,128)(2,1)} %bitcast.83, f32[2,13,256]{2,1,0:T(8,128)} %get-tuple-element.28, pred[2,13,256]{2,1,0:T(8,128)(4,1)} %copy.164), kind=kLoop, calls=%fused_computation.14 | loop fusion | flops 1253376 | bytes 770560 | tf_op jit(solution)/shard_map/reduce_sum | solution.py:63
  211.1 0.7 copy.170
  211.8 15.4 %gather_fusion.2 = bf16[6656,48]{1,0:T(8,128)(2,1)} fusion(bf16[48,8192]{0,1:T(8,128)(2,1)S(1)} %bitcast.72, s32[7168]{0:T(1024)} %pad_clamp_fusion.1), kind=kCustom, calls=%fused_computation.2.clone | custom fusion | bytes 1304576 | tf_op jit(solution)/shard_map/jit(_take)/gather | solution.py:59
  227.2 5.4 %multiply_reduce_fusion.5 = f32[48,2,256]{0,2,1:T(8,128)S(1)} fusion(bf16[2,13,256,48]{3,2,1,0:T(8,128)(2,1)} %bitcast.85, f32[2,13,256]{2,1,0:T(8,128)} %get-tuple-element.27, pred[2,13,256]{2,1,0:T(8,128)(4,1)} %copy.172), kind=kLoop, calls=%fused_computation.13 | loop fusion | flops 1253376 | bytes 770560 | tf_op jit(solution)/shard_map/reduce_sum | solution.py:63
  232.6 0.8 copy.177
  233.4 15.5 %gather_fusion.3 = bf16[6656,48]{1,0:T(8,128)(2,1)} fusion(bf16[48,8192]{0,1:T(8,128)(2,1)S(1)} %bitcast.73, s32[7168]{0:T(1024)} %pad_clamp_fusion), kind=kCustom, calls=%fused_computation.3.clone | custom fusion | bytes 1304576 | tf_op jit(solution)/shard_map/jit(_take)/gather | solution.py:59
  248.9 5.4 %multiply_reduce_fusion.4 = f32[48,2,256]{0,2,1:T(8,128)S(1)} fusion(bf16[2,13,256,48]{3,2,1,0:T(8,128)(2,1)} %bitcast.82, f32[2,13,256]{2,1,0:T(8,128)S(1)} %copy-done.11, pred[2,13,256]{2,1,0:T(8,128)(4,1)S(1)} %copy-done.22), kind=kLoop, calls=%fused_computation.12 | loop fusion | flops 1253376 | bytes 770560 | tf_op jit(solution)/shard_map/reduce_sum | solution.py:63
  254.3 0.1 copy.184
  254.5 21.0 %all_gather.7 = bf16[48,32,256]{2,0,1:T(8,128)(2,1)} all-gather(bf16[48,2,256]{2,0,1:T(8,128)(2,1)S(1)} %add_convert_fusion), channel_id=1, replica_groups=mesh['region'=2,'shard'=16] {'shard'}, dimensions={1}, use_global_device_ids=true | all-gather | bytes 835584 | tf_op jit(solution)/shard_map/all_gather | solution.py:49
  275.5 2.0 copy.185
  277.5 14.2 %gather_fusion.4 = bf16[6656,48]{1,0:T(8,128)(2,1)} fusion(bf16[48,8192]{0,1:T(8,128)(2,1)S(1)} %bitcast.74, s32[7168]{0:T(1024)S(1)} %copy-done.7), kind=kCustom, calls=%fused_computation.4.clone | custom fusion | bytes 1304576 | tf_op jit(solution)/shard_map/jit(_take)/gather | solution.py:59
  291.6 14.1 %gather_fusion.5 = bf16[6656,48]{1,0:T(8,128)(2,1)} fusion(bf16[48,8192]{0,1:T(8,128)(2,1)S(1)} %bitcast.75, s32[7168]{0:T(1024)S(1)} %copy-done.8), kind=kCustom, calls=%fused_computation.5.clone | custom fusion | bytes 1304576 | tf_op jit(solution)/shard_map/jit(_take)/gather | solution.py:59
  305.8 14.1 %gather_fusion.6 = bf16[6656,48]{1,0:T(8,128)(2,1)} fusion(bf16[48,8192]{0,1:T(8,128)(2,1)S(1)} %bitcast.76, s32[7168]{0:T(1024)S(1)} %copy-done.9), kind=kCustom, calls=%fused_computation.6.clone | custom fusion | bytes 1304576 | tf_op jit(solution)/shard_map/jit(_take)/gather | solution.py:59
  319.9 14.2 %gather_fusion.7 = bf16[6656,48]{1,0:T(8,128)(2,1)} fusion(bf16[48,8192]{0,1:T(8,128)(2,1)S(1)} %bitcast.77, s32[7168]{0:T(1024)S(1)} %copy-done.10), kind=kCustom, calls=%fused_computation.7.clone | custom fusion | bytes 1304576 | tf_op jit(solution)/shard_map/jit(_take)/gather | solution.py:59
  334.1 5.5 %multiply_reduce_fusion.3 = f32[48,2,256]{0,2,1:T(8,128)S(1)} fusion(bf16[2,13,256,48]{3,2,1,0:T(8,128)(2,1)} %bitcast.81, f32[2,13,256]{2,1,0:T(8,128)S(1)} %copy-done.15, pred[2,13,256]{2,1,0:T(8,128)(4,1)S(1)} %copy-done.19), kind=kLoop, calls=%fused_computation.11 | loop fusion | flops 1253376 | bytes 770560 | tf_op jit(solution)/shard_map/reduce_sum | solution.py:63
  339.6 0.1 copy.189
  339.7 2.4 multiply_reduce_fusion.2
  342.2 0.1 copy.190
  342.3 5.4 %multiply_reduce_fusion.1 = f32[48,2,256]{0,2,1:T(8,128)S(1)} fusion(bf16[2,13,256,48]{3,2,1,0:T(8,128)(2,1)} %bitcast.79, f32[2,13,256]{2,1,0:T(8,128)S(1)} %copy-done.12, pred[2,13,256]{2,1,0:T(8,128)(4,1)S(1)} %copy-done.21), kind=kLoop, calls=%fused_computation.9 | loop fusion | flops 1253376 | bytes 770560 | tf_op jit(solution)/shard_map/reduce_sum | solution.py:63
  347.7 0.1 copy.193
  347.9 2.4 multiply_reduce_fusion
  350.3 0.1 copy.196
  350.5 0.7 convert_add_fusion.1
  (72 shorter events, 0.4 us)
Async XLA Ops:
  6.5 2.0 copy-start
  6.5 4.4 %copy-start.25 = (s32[2,13]{1,0:T(2,128)S(1)}, s32[2,13]{1,0:T(2,128)}, u32[]{:S(2)}) copy-start(s32[2,13]{1,0:T(2,128)} %param.14) | copy-start | bytes 316
  6.5 4.4 %copy-start.24 = (s32[2,13]{1,0:T(2,128)S(1)}, s32[2,13]{1,0:T(2,128)}, u32[]{:S(2)}) copy-start(s32[2,13]{1,0:T(2,128)} %param.15) | copy-start | bytes 316
  6.5 4.4 %copy-start.17 = (s32[2,13,4,256]{3,2,1,0:T(4,128)S(1)}, s32[2,13,4,256]{3,2,1,0:T(4,128)}, u32[]{:S(2)}) copy-start(s32[2,13,4,256]{3,2,1,0:T(4,128)} %param.13) | copy-start | bytes 319492
  6.5 133.7 %all-reduce.2.cloned.1.call-start = ((), (), s32[]{:S(2)}) async-start(), calls=%async_computation | async-start | bytes 393216 | tf_op jit(solution)/shard_map/psum | solution.py:32
  8.6 2.7 copy-start.16
  10.9 129.4 %copy-start.3 = (bf16[48,1024]{1,0:T(8,128)(2,1)S(1)}, bf16[48,1024]{1,0:T(8,128)(2,1)}, u32[]{:S(2)}) copy-start(bf16[48,1024]{1,0:T(8,128)(2,1)} %param.9) | copy-start | bytes 294916
  11.3 159.5 %copy-start.6 = (s32[7168]{0:T(1024)}, s32[7168]{0:T(1024)S(1)}, u32[]{:S(2)}) copy-start(s32[7168]{0:T(1024)S(1)} %pad_clamp_fusion.3) | copy-start | bytes 86020
  11.3 173.6 %copy-start.18 = (pred[2,13,256]{2,1,0:T(8,128)(4,1)}, pred[2,13,256]{2,1,0:T(8,128)(4,1)S(1)}, u32[]{:S(2)}) copy-start(pred[2,13,256]{2,1,0:T(8,128)(4,1)S(1)} %copy.154) | copy-start | bytes 19972
  15.2 169.7 %copy-start.14 = (f32[2,13,256]{2,1,0:T(8,128)}, f32[2,13,256]{2,1,0:T(8,128)S(1)}, u32[]{:S(2)}) copy-start(f32[2,13,256]{2,1,0:T(8,128)S(1)} %get-tuple-element.29) | copy-start | bytes 79876
  233.4 15.5 %copy-start.11 = (f32[2,13,256]{2,1,0:T(8,128)S(1)}, f32[2,13,256]{2,1,0:T(8,128)}, u32[]{:S(2)}) copy-start(f32[2,13,256]{2,1,0:T(8,128)} %get-tuple-element.26) | copy-start | bytes 79876
  233.4 15.5 %copy-start.22 = (pred[2,13,256]{2,1,0:T(8,128)(4,1)S(1)}, pred[2,13,256]{2,1,0:T(8,128)(4,1)}, u32[]{:S(2)}) copy-start(pred[2,13,256]{2,1,0:T(8,128)(4,1)} %copy.179) | copy-start | bytes 19972
  248.9 5.5 %copy-start.4 = (f32[48,2,256]{2,0,1:T(8,128)S(1)}, f32[48,2,256]{2,0,1:T(8,128)}, u32[]{:S(2)}) copy-start(f32[48,2,256]{2,0,1:T(8,128)} %copy.170) | copy-start | bytes 294916
  248.9 5.5 %copy-start.5 = (f32[48,2,256]{2,0,1:T(8,128)S(1)}, f32[48,2,256]{2,0,1:T(8,128)}, u32[]{:S(2)}) copy-start(f32[48,2,256]{2,0,1:T(8,128)} %copy.177) | copy-start | bytes 294916
  254.4 23.0 %copy-start.7 = (s32[7168]{0:T(1024)S(1)}, s32[7168]{0:T(1024)}, u32[]{:S(2)}) copy-start(s32[7168]{0:T(1024)} %copy-done.6) | copy-start | bytes 86020
  277.5 14.2 %copy-start.8 = (s32[7168]{0:T(1024)S(1)}, s32[7168]{0:T(1024)}, u32[]{:S(2)}) copy-start(s32[7168]{0:T(1024)} %pad_clamp_fusion.2) | copy-start | bytes 86020
  291.6 14.1 %copy-start.9 = (s32[7168]{0:T(1024)S(1)}, s32[7168]{0:T(1024)}, u32[]{:S(2)}) copy-start(s32[7168]{0:T(1024)} %pad_clamp_fusion.1) | copy-start | bytes 86020
  305.8 14.2 %copy-start.10 = (s32[7168]{0:T(1024)S(1)}, s32[7168]{0:T(1024)}, u32[]{:S(2)}) copy-start(s32[7168]{0:T(1024)} %pad_clamp_fusion) | copy-start | bytes 86020
  319.9 14.2 %copy-start.15 = (f32[2,13,256]{2,1,0:T(8,128)S(1)}, f32[2,13,256]{2,1,0:T(8,128)}, u32[]{:S(2)}) copy-start(f32[2,13,256]{2,1,0:T(8,128)} %copy-done.14) | copy-start | bytes 79876
  319.9 14.2 %copy-start.19 = (pred[2,13,256]{2,1,0:T(8,128)(4,1)S(1)}, pred[2,13,256]{2,1,0:T(8,128)(4,1)}, u32[]{:S(2)}) copy-start(pred[2,13,256]{2,1,0:T(8,128)(4,1)} %copy-done.18) | copy-start | bytes 19972
  334.1 5.6 %copy-start.2 = (bf16[6656,48]{1,0:T(8,128)(2,1)S(1)}, bf16[6656,48]{1,0:T(8,128)(2,1)}, u32[]{:S(2)}) copy-start(bf16[6656,48]{1,0:T(8,128)(2,1)} %gather_fusion.5) | copy-start | bytes 1916932
  334.1 5.6 %copy-start.13 = (f32[2,13,256]{2,1,0:T(8,128)S(1)}, f32[2,13,256]{2,1,0:T(8,128)}, u32[]{:S(2)}) copy-start(f32[2,13,256]{2,1,0:T(8,128)} %get-tuple-element.28) | copy-start | bytes 79876
  334.1 5.6 %copy-start.20 = (pred[2,13,256]{2,1,0:T(8,128)(4,1)S(1)}, pred[2,13,256]{2,1,0:T(8,128)(4,1)}, u32[]{:S(2)}) copy-start(pred[2,13,256]{2,1,0:T(8,128)(4,1)} %copy.164) | copy-start | bytes 19972
  339.6 2.7 copy-start.12
  339.6 2.7 copy-start.21
  342.1 5.7 %copy-start.1 = (bf16[6656,48]{1,0:T(8,128)(2,1)S(1)}, bf16[6656,48]{1,0:T(8,128)(2,1)}, u32[]{:S(2)}) copy-start(bf16[6656,48]{1,0:T(8,128)(2,1)} %gather_fusion.7) | copy-start | bytes 1916932
  342.2 5.7 %copy-start.23 = (pred[2,13,256]{2,1,0:T(8,128)(4,1)S(1)}, pred[2,13,256]{2,1,0:T(8,128)(4,1)}, u32[]{:S(2)}) copy-start(pred[2,13,256]{2,1,0:T(8,128)(4,1)} %copy.179) | copy-start | bytes 19972
Sparse Core Ops, SparseCore 0:
  12.9 127.3 all-reduce.1
where the time goes:
time: 360 us; the launch traced here: 358 us
  local copies, waits for them, and re-layouts  125 us (35%)
  waiting for transfers between devices  124 us (34%)
  blocking collectives  46.9 us (13%)
  other arithmetic  44.3 us (12%)
  between operations  13.9 us (4%)
  matrix products  3.67 us (1%)
    psum x1, waiting for transfers between devices, per_device(): lax.psum(local_term, ('region', 'shard')) + unit_query.astype(jnp.float32)  124 us
    gather x8, local copies, waits for them, and re-layouts, spread(): reached = jnp.take(flat, flat_columns[:, :, edge, :], axis=1)  117 us
    all_gather x2, blocking collectives, fetch_blocks(): region_blocks = lax.all_gather(current, 'shard', axis=1, tiled=True)  46.9 us
    reduce_sum x8, other arithmetic, spread(): total = total + jnp.sum(scaled, axis=2)  37.2 us
  transfers between devices with their start and end apart: 1, of which 1 were waited for; matrix products, arithmetic and copies ran while one was open for 1% of the time, Pallas kernels for 0%

commit v1 on v0

--- a/solution.py
+++ b/solution.py
@@ -46,7 +46,24 @@
     sources = owners * blocks_dev + block_ids
 
     def fetch_blocks(current):
-        region_blocks = lax.all_gather(current, "shard", axis=1, tiled=True)
+        ways, here, step = (lax.axis_size("shard"), lax.axis_index("shard"), current.shape[1])
+        shape = [n * ways if d == 1 else n for d, n in enumerate(current.shape)]
+        region_blocks = lax.dynamic_update_slice_in_dim(
+            jnp.zeros(shape, current.dtype), current, here * step, axis=1
+        )
+        going_up = going_down = current
+        for far in range(1, ways // 2 + 1):
+            going_up = lax.ppermute(going_up, "shard", [(d, (d + 1) % ways) for d in range(ways)])
+            region_blocks = lax.dynamic_update_slice_in_dim(
+                region_blocks, going_up, (here - far) % ways * step, axis=1
+            )
+            if 2 * far < ways:
+                going_down = lax.ppermute(
+                    going_down, "shard", [(d, (d - 1) % ways) for d in range(ways)]
+                )
+                region_blocks = lax.dynamic_update_slice_in_dim(
+                    region_blocks, going_down, (here + far) % ways * step, axis=1
+                )
         return region_blocks.reshape(query_count, -1)
 
     column_base = (sources * block_rows).reshape(blocks_dev, tile_count, 1, 1)

time: 360 us -> 417 us (1.16)
  starting transfers between devices: 0.03 us -> 63.2 us
  blocking collectives: 46.9 us -> 0 us
  waiting for transfers between devices: 124 us -> 164 us
  local copies, waits for them, and re-layouts: 125 us -> 133 us
  other arithmetic: 44.3 us -> 37 us
    ppermute x0 -> x30, starting transfers between devices: none -> 63.2 us  [the longest x14 62.7 us: fetch_blocks(): lax.ppermute(going_down, 'shard', [(d, (d - 1) % ways) for d in range(way...]
    all_gather x2 -> x0, blocking collectives: 46.9 us -> none  [fetch_blocks(): region_blocks = lax.all_gather(current, 'shard', axis=1, tiled=True)]
    ppermute x0 -> x30, waiting for transfers between devices: none -> 39 us  [the longest x16 39 us: fetch_blocks(): lax.ppermute(going_up, 'shard', [(d, (d + 1) % ways) for d in range(ways)])]
    ppermute x0 -> x15, local copies, waits for them, and re-layouts: none -> 13.9 us  [the longest x8 7.41 us: fetch_blocks(): lax.ppermute(going_up, 'shard', [(d, (d + 1) % ways) for d in range(ways)])]
    reduce_sum x8, other arithmetic: 37.2 us -> 31.5 us  [spread(): total = total + jnp.sum(scaled, axis=2)]
  transfers between devices with their start and end apart: 1 -> 31, of which waited for: 1 -> 17; matrix products, arithmetic and copies ran while one was open for 1% -> 4% of each run, Pallas kernels for 0% -> 0%
where the time goes in v1:
time: 417 us; the launch traced here: 415 us
  waiting for transfers between devices  164 us (39%)
  local copies, waits for them, and re-layouts  133 us (32%)
  starting transfers between devices  63.2 us (15%)
  other arithmetic  37 us (9%)
  between operations  14.5 us (3%)
    psum x1, waiting for transfers between devices, per_device(): lax.psum(local_term, ('region', 'shard')) + unit_query.astype(jnp.float32)  125 us
    gather x8, local copies, waits for them, and re-layouts, spread(): reached = jnp.take(flat, flat_columns[:, :, edge, :], axis=1)  113 us
    ppermute x14, starting transfers between devices, fetch_blocks(): lax.ppermute(going_down, 'shard', [(d, (d - 1) % ways) for d in range(way...  62.7 us
    ppermute x16, waiting for transfers between devices, fetch_blocks(): lax.ppermute(going_up, 'shard', [(d, (d + 1) % ways) for d in range(ways)])  39 us
    reduce_sum x8, other arithmetic, spread(): total = total + jnp.sum(scaled, axis=2)  31.5 us
  transfers between devices with their start and end apart: 31, of which 17 were waited for; matrix products, arithmetic and copies ran while one was open for 4% of the time, Pallas kernels for 0%

profile of v1, /device:TPU:0, one launch (start us, length us, event | category | flops | bytes accessed | tf_op | source)
XLA Modules:
  0.0 415.3 jit_solution(2922876308512405050)
XLA Ops:
  8.6 2.3 fusion.8
  15.5 124.8 %all-reduce.2.cloned.1.call-done = f32[48,1024]{1,0:T(8,128)} async-done(((f32[48,1024]{1,0:T(8,128)}), f32[48,1024]{1,0:T(8,128)}) %all-reduce.2.cloned.1.call-update) | async-done | bytes 196624 | tf_op jit(solution)/shard_map/psum | solution.py:32
  140.3 1.1 multiply_reduce_fusion.8
  141.5 1.4 fusion
  144.5 4.4 %collective-permute-start.1 = (bf16[48,2,256]{2,1,0:T(2,128)(2,1)}, bf16[48,2,256]{2,1,0:T(2,128)(2,1)}, u32[]{:S(2)}, u32[]{:S(2)}) collective-permute-start(bf16[48,2,256]{2,1,0:T(2,128)(2,1)} %reshape.74), channel_id=1, source_target_pairs={{0,15},{1,0},{2,1},{3,2},{4,3},{5,4},{6,5},{7,6},{8,7},{9,8},{10,9... | collective-permute-start | bytes 147464 | tf_op jit(solution)/shard_map/ppermute | solution.py:61
  149.4 1.6 collective-permute-done
  153.0 4.5 %collective-permute-start.3 = (bf16[48,2,256]{2,1,0:T(2,128)(2,1)}, bf16[48,2,256]{2,1,0:T(2,128)(2,1)}, u32[]{:S(2)}, u32[]{:S(2)}) collective-permute-start(bf16[48,2,256]{2,1,0:T(2,128)(2,1)} %collective-permute-done.1), channel_id=1, source_target_pairs={{0,15},{1,0},{2,1},{3,2},{4,3},{5,4},{6,5},{7,6},{8,7},{9,8},{10,9... | collective-permute-start | bytes 147464 | tf_op jit(solution)/shard_map/ppermute | solution.py:61
  157.5 1.1 collective-permute-done.2
  160.6 4.5 %collective-permute-start.5 = (bf16[48,2,256]{2,1,0:T(2,128)(2,1)}, bf16[48,2,256]{2,1,0:T(2,128)(2,1)}, u32[]{:S(2)}, u32[]{:S(2)}) collective-permute-start(bf16[48,2,256]{2,1,0:T(2,128)(2,1)} %collective-permute-done.3), channel_id=1, source_target_pairs={{0,15},{1,0},{2,1},{3,2},{4,3},{5,4},{6,5},{7,6},{8,7},{9,8},{10,9... | collective-permute-start | bytes 147464 | tf_op jit(solution)/shard_map/ppermute | solution.py:61
  165.0 1.1 collective-permute-done.4
  168.1 4.5 %collective-permute-start.7 = (bf16[48,2,256]{2,1,0:T(2,128)(2,1)}, bf16[48,2,256]{2,1,0:T(2,128)(2,1)}, u32[]{:S(2)}, u32[]{:S(2)}) collective-permute-start(bf16[48,2,256]{2,1,0:T(2,128)(2,1)} %collective-permute-done.5), channel_id=1, source_target_pairs={{0,15},{1,0},{2,1},{3,2},{4,3},{5,4},{6,5},{7,6},{8,7},{9,8},{10,9... | collective-permute-start | bytes 147464 | tf_op jit(solution)/shard_map/ppermute | solution.py:61
  172.6 1.1 collective-permute-done.6
  175.6 4.5 %collective-permute-start.9 = (bf16[48,2,256]{2,1,0:T(2,128)(2,1)}, bf16[48,2,256]{2,1,0:T(2,128)(2,1)}, u32[]{:S(2)}, u32[]{:S(2)}) collective-permute-start(bf16[48,2,256]{2,1,0:T(2,128)(2,1)} %collective-permute-done.7), channel_id=1, source_target_pairs={{0,15},{1,0},{2,1},{3,2},{4,3},{5,4},{6,5},{7,6},{8,7},{9,8},{10,9... | collective-permute-start | bytes 147464 | tf_op jit(solution)/shard_map/ppermute | solution.py:61
  180.1 1.1 collective-permute-done.8
  183.2 4.5 %collective-permute-start.11 = (bf16[48,2,256]{2,1,0:T(2,128)(2,1)}, bf16[48,2,256]{2,1,0:T(2,128)(2,1)}, u32[]{:S(2)}, u32[]{:S(2)}) collective-permute-start(bf16[48,2,256]{2,1,0:T(2,128)(2,1)} %collective-permute-done.9), channel_id=1, source_target_pairs={{0,15},{1,0},{2,1},{3,2},{4,3},{5,4},{6,5},{7,6},{8,7},{9,8},{10,9... | collective-permute-start | bytes 147464 | tf_op jit(solution)/shard_map/ppermute | solution.py:61
  190.7 4.5 %collective-permute-start.13 = (bf16[48,2,256]{2,1,0:T(2,128)(2,1)}, bf16[48,2,256]{2,1,0:T(2,128)(2,1)}, u32[]{:S(2)}, u32[]{:S(2)}) collective-permute-start(bf16[48,2,256]{2,1,0:T(2,128)(2,1)} %collective-permute-done.11), channel_id=1, source_target_pairs={{0,15},{1,0},{2,1},{3,2},{4,3},{5,4},{6,5},{7,6},{8,7},{9,8},{10,9... | collective-permute-start | bytes 147464 | tf_op jit(solution)/shard_map/ppermute | solution.py:61
  198.3 5.5 %collective-permute-done.14 = bf16[48,2,256]{2,1,0:T(2,128)(2,1)} collective-permute-done((bf16[48,2,256]{2,1,0:T(2,128)(2,1)}, bf16[48,2,256]{2,1,0:T(2,128)(2,1)}, u32[]{:S(2)}, u32[]{:S(2)}) %collective-permute-start.14) | collective-permute-done | bytes 49184 | tf_op jit(solution)/shard_map/ppermute | solution.py:56
  204.8 14.1 %gather_fusion.2 = bf16[6656,48]{1,0:T(8,128)(2,1)} fusion(bf16[48,8192]{0,1:T(8,128)(2,1)S(1)} %bitcast.66, s32[7168]{0:T(1024)S(1)} %pad_clamp_fusion.1), kind=kCustom, calls=%fused_computation.2.clone | custom fusion | bytes 1304576 | tf_op jit(solution)/shard_map/jit(_take)/gather | solution.py:76
  218.9 14.2 %gather_fusion.1 = bf16[6656,48]{1,0:T(8,128)(2,1)} fusion(bf16[48,8192]{0,1:T(8,128)(2,1)S(1)} %bitcast.67, s32[7168]{0:T(1024)S(1)} %pad_clamp_fusion.2), kind=kCustom, calls=%fused_computation.1.clone | custom fusion | bytes 1304576 | tf_op jit(solution)/shard_map/jit(_take)/gather | solution.py:76
  233.1 14.1 %gather_fusion = bf16[6656,48]{1,0:T(8,128)(2,1)} fusion(bf16[48,8192]{0,1:T(8,128)(2,1)S(1)} %bitcast.68, s32[7168]{0:T(1024)S(1)} %pad_clamp_fusion.3), kind=kCustom, calls=%fused_computation.clone | custom fusion | bytes 1304576 | tf_op jit(solution)/shard_map/jit(_take)/gather | solution.py:76
  247.2 14.2 %gather_fusion.3 = bf16[6656,48]{1,0:T(8,128)(2,1)} fusion(bf16[48,8192]{0,1:T(8,128)(2,1)S(1)} %bitcast.69, s32[7168]{0:T(1024)S(1)} %pad_clamp_fusion), kind=kCustom, calls=%fused_computation.3.clone | custom fusion | bytes 1304576 | tf_op jit(solution)/shard_map/jit(_take)/gather | solution.py:76
  261.4 5.5 %multiply_reduce_fusion.5 = f32[48,2,256]{0,2,1:T(8,128)S(1)} fusion(bf16[2,13,256,48]{3,2,1,0:T(8,128)(2,1)} %bitcast.77, f32[2,13,256]{2,1,0:T(8,128)S(1)} %copy-done.7, pred[2,13,256]{2,1,0:T(8,128)(4,1)S(1)} %copy-done.13), kind=kLoop, calls=%fused_computation.13 | loop fusion | flops 1253376 | bytes 770560 | tf_op jit(solution)/shard_map/reduce_sum | solution.py:80
  266.9 5.5 %multiply_reduce_fusion.6 = f32[48,2,256]{0,2,1:T(8,128)S(1)} fusion(bf16[2,13,256,48]{3,2,1,0:T(8,128)(2,1)} %bitcast.76, f32[2,13,256]{2,1,0:T(8,128)S(1)} %copy-done.8, pred[2,13,256]{2,1,0:T(8,128)(4,1)S(1)} %copy-done.14), kind=kLoop, calls=%fused_computation.14 | loop fusion | flops 1253376 | bytes 770560 | tf_op jit(solution)/shard_map/reduce_sum | solution.py:80
  272.4 2.4 multiply_reduce_fusion.7
  274.9 2.4 multiply_reduce_fusion.4
  277.9 4.4 %collective-permute-start.16 = (bf16[48,2,256]{0,2,1:T(8,128)(2,1)S(1)}, bf16[48,2,256]{0,2,1:T(8,128)(2,1)S(1)}, u32[]{:S(2)}, u32[]{:S(2)}) collective-permute-start(bf16[48,2,256]{0,2,1:T(8,128)(2,1)S(1)} %get-tuple-element.7), channel_id=1, source_target_pairs={{0,15},{1,0},{2,1},{3,2},{4,3},{5,4},{6,5},{7,6},{8,7},{9,8},{10,9... | collective-permute-start | bytes 147464 | tf_op jit(solution)/shard_map/ppermute | solution.py:61
  282.3 2.7 collective-permute-done.15
  285.1 4.5 %collective-permute-start.18 = (bf16[48,2,256]{0,2,1:T(8,128)(2,1)S(1)}, bf16[48,2,256]{0,2,1:T(8,128)(2,1)S(1)}, u32[]{:S(2)}, u32[]{:S(2)}) collective-permute-start(bf16[48,2,256]{0,2,1:T(8,128)(2,1)S(1)} %collective-permute-done.16), channel_id=1, source_target_pairs={{0,15},{1,0},{2,1},{3,2},{4,3},{5,4},{6,5},{7,6},{8,7},{9,8},{10,9... | collective-permute-start | bytes 147464 | tf_op jit(solution)/shard_map/ppermute | solution.py:61
  289.6 2.6 collective-permute-done.17
  292.3 4.5 %collective-permute-start.20 = (bf16[48,2,256]{0,2,1:T(8,128)(2,1)S(1)}, bf16[48,2,256]{0,2,1:T(8,128)(2,1)S(1)}, u32[]{:S(2)}, u32[]{:S(2)}) collective-permute-start(bf16[48,2,256]{0,2,1:T(8,128)(2,1)S(1)} %collective-permute-done.18), channel_id=1, source_target_pairs={{0,15},{1,0},{2,1},{3,2},{4,3},{5,4},{6,5},{7,6},{8,7},{9,8},{10,9... | collective-permute-start | bytes 147464 | tf_op jit(solution)/shard_map/ppermute | solution.py:61
  296.8 2.6 collective-permute-done.19
  299.5 4.5 %collective-permute-start.22 = (bf16[48,2,256]{0,2,1:T(8,128)(2,1)S(1)}, bf16[48,2,256]{0,2,1:T(8,128)(2,1)S(1)}, u32[]{:S(2)}, u32[]{:S(2)}) collective-permute-start(bf16[48,2,256]{0,2,1:T(8,128)(2,1)S(1)} %collective-permute-done.20), channel_id=1, source_target_pairs={{0,15},{1,0},{2,1},{3,2},{4,3},{5,4},{6,5},{7,6},{8,7},{9,8},{10,9... | collective-permute-start | bytes 147464 | tf_op jit(solution)/shard_map/ppermute | solution.py:61
  304.0 2.6 collective-permute-done.21
  306.7 4.5 %collective-permute-start.24 = (bf16[48,2,256]{0,2,1:T(8,128)(2,1)S(1)}, bf16[48,2,256]{0,2,1:T(8,128)(2,1)S(1)}, u32[]{:S(2)}, u32[]{:S(2)}) collective-permute-start(bf16[48,2,256]{0,2,1:T(8,128)(2,1)S(1)} %collective-permute-done.22), channel_id=1, source_target_pairs={{0,15},{1,0},{2,1},{3,2},{4,3},{5,4},{6,5},{7,6},{8,7},{9,8},{10,9... | collective-permute-start | bytes 147464 | tf_op jit(solution)/shard_map/ppermute | solution.py:61
  311.2 2.6 collective-permute-done.23
  313.9 4.5 %collective-permute-start.26 = (bf16[48,2,256]{0,2,1:T(8,128)(2,1)S(1)}, bf16[48,2,256]{0,2,1:T(8,128)(2,1)S(1)}, u32[]{:S(2)}, u32[]{:S(2)}) collective-permute-start(bf16[48,2,256]{0,2,1:T(8,128)(2,1)S(1)} %collective-permute-done.24), channel_id=1, source_target_pairs={{0,15},{1,0},{2,1},{3,2},{4,3},{5,4},{6,5},{7,6},{8,7},{9,8},{10,9... | collective-permute-start | bytes 147464 | tf_op jit(solution)/shard_map/ppermute | solution.py:61
  318.4 2.6 collective-permute-done.25
  321.1 4.5 %collective-permute-start.28 = (bf16[48,2,256]{0,2,1:T(8,128)(2,1)S(1)}, bf16[48,2,256]{0,2,1:T(8,128)(2,1)S(1)}, u32[]{:S(2)}, u32[]{:S(2)}) collective-permute-start(bf16[48,2,256]{0,2,1:T(8,128)(2,1)S(1)} %collective-permute-done.26), channel_id=1, source_target_pairs={{0,15},{1,0},{2,1},{3,2},{4,3},{5,4},{6,5},{7,6},{8,7},{9,8},{10,9... | collective-permute-start | bytes 147464 | tf_op jit(solution)/shard_map/ppermute | solution.py:61
  325.6 2.5 collective-permute-done.27
  328.2 7.0 %collective-permute-done.29 = bf16[48,2,256]{0,2,1:T(8,128)(2,1)S(1)} collective-permute-done((bf16[48,2,256]{0,2,1:T(8,128)(2,1)S(1)}, bf16[48,2,256]{0,2,1:T(8,128)(2,1)S(1)}, u32[]{:S(2)}, u32[]{:S(2)}) %collective-permute-start.29) | collective-permute-done | bytes 49184 | tf_op jit(solution)/shard_map/ppermute | solution.py:56
  335.2 14.1 %gather_fusion.6 = bf16[6656,48]{1,0:T(8,128)(2,1)} fusion(bf16[48,8192]{0,1:T(8,128)(2,1)S(1)} %bitcast.62, s32[7168]{0:T(1024)S(1)} %pad_clamp_fusion.1), kind=kCustom, calls=%fused_computation.6.clone | custom fusion | bytes 1304576 | tf_op jit(solution)/shard_map/jit(_take)/gather | solution.py:76
  349.4 14.1 %gather_fusion.5 = bf16[6656,48]{1,0:T(8,128)(2,1)} fusion(bf16[48,8192]{0,1:T(8,128)(2,1)S(1)} %bitcast.63, s32[7168]{0:T(1024)S(1)} %pad_clamp_fusion.2), kind=kCustom, calls=%fused_computation.5.clone | custom fusion | bytes 1304576 | tf_op jit(solution)/shard_map/jit(_take)/gather | solution.py:76
  363.5 14.2 %gather_fusion.4 = bf16[6656,48]{1,0:T(8,128)(2,1)} fusion(bf16[48,8192]{0,1:T(8,128)(2,1)S(1)} %bitcast.64, s32[7168]{0:T(1024)S(1)} %pad_clamp_fusion.3), kind=kCustom, calls=%fused_computation.4.clone | custom fusion | bytes 1304576 | tf_op jit(solution)/shard_map/jit(_take)/gather | solution.py:76
  377.7 14.1 %gather_fusion.7 = bf16[6656,48]{1,0:T(8,128)(2,1)} fusion(bf16[48,8192]{0,1:T(8,128)(2,1)S(1)} %bitcast.65, s32[7168]{0:T(1024)S(1)} %pad_clamp_fusion), kind=kCustom, calls=%fused_computation.7.clone | custom fusion | bytes 1304576 | tf_op jit(solution)/shard_map/jit(_take)/gather | solution.py:76
  391.8 5.5 %multiply_reduce_fusion.1 = f32[48,2,256]{0,2,1:T(8,128)S(1)} fusion(bf16[2,13,256,48]{3,2,1,0:T(8,128)(2,1)} %bitcast.73, f32[2,13,256]{2,1,0:T(8,128)S(1)} %copy-done.7, pred[2,13,256]{2,1,0:T(8,128)(4,1)S(1)} %copy-done.13), kind=kLoop, calls=%fused_computation.9 | loop fusion | flops 1253376 | bytes 770560 | tf_op jit(solution)/shard_map/reduce_sum | solution.py:80
  397.3 5.5 %multiply_reduce_fusion.2 = f32[48,2,256]{0,2,1:T(8,128)S(1)} fusion(bf16[2,13,256,48]{3,2,1,0:T(8,128)(2,1)} %bitcast.72, f32[2,13,256]{2,1,0:T(8,128)S(1)} %copy-done.8, pred[2,13,256]{2,1,0:T(8,128)(4,1)S(1)} %copy-done.14), kind=kLoop, calls=%fused_computation.10 | loop fusion | flops 1253376 | bytes 770560 | tf_op jit(solution)/shard_map/reduce_sum | solution.py:80
  402.8 2.4 multiply_reduce_fusion.3
  405.2 2.4 multiply_reduce_fusion
  (155 shorter events, 27.0 us)
Async XLA Ops:
  6.5 4.7 %copy-start.18 = (s32[2,13]{1,0:T(2,128)S(1)}, s32[2,13]{1,0:T(2,128)}, u32[]{:S(2)}) copy-start(s32[2,13]{1,0:T(2,128)} %param.14) | copy-start | bytes 316
  6.5 4.7 %copy-start.17 = (s32[2,13]{1,0:T(2,128)S(1)}, s32[2,13]{1,0:T(2,128)}, u32[]{:S(2)}) copy-start(s32[2,13]{1,0:T(2,128)} %param.15) | copy-start | bytes 316
  6.5 4.7 %copy-start.12 = (s32[2,13,4,256]{3,2,1,0:T(4,128)S(1)}, s32[2,13,4,256]{3,2,1,0:T(4,128)}, u32[]{:S(2)}) copy-start(s32[2,13,4,256]{3,2,1,0:T(4,128)} %param.13) | copy-start | bytes 319492
  6.5 5.6 %copy-start.9 = (bf16[2,13,4,256]{3,2,1,0:T(4,128)(2,1)S(1)}, bf16[2,13,4,256]{3,2,1,0:T(4,128)(2,1)}, u32[]{:S(2)}) copy-start(bf16[2,13,4,256]{3,2,1,0:T(4,128)(2,1)} %param.12) | copy-start | bytes 159748
  6.5 133.8 %all-reduce.2.cloned.1.call-start = ((), (), s32[]{:S(2)}) async-start(), calls=%async_computation | async-start | bytes 393216 | tf_op jit(solution)/shard_map/psum | solution.py:32
  8.6 131.7 %copy-start.5 = (bf16[48,1024]{1,0:T(8,128)(2,1)S(1)}, bf16[48,1024]{1,0:T(8,128)(2,1)}, u32[]{:S(2)}) copy-start(bf16[48,1024]{1,0:T(8,128)(2,1)} %param.9) | copy-start | bytes 294916
  144.4 6.6 %collective-permute-start = (bf16[48,2,256]{2,1,0:T(2,128)(2,1)}, bf16[48,2,256]{2,1,0:T(2,128)(2,1)}, u32[]{:S(2)}, u32[]{:S(2)}) collective-permute-start(bf16[48,2,256]{2,1,0:T(2,128)(2,1)} %reshape.74), channel_id=1, source_target_pairs={{0,1},{1,2},{2,3},{3,4},{4,5},{5,6},{6,7},{7,8},{8,9},{9,10},{10,1... | collective-permute-start | bytes 147464 | tf_op jit(solution)/shard_map/ppermute | solution.py:56
  144.5 7.5 %collective-permute-start.1 = (bf16[48,2,256]{2,1,0:T(2,128)(2,1)}, bf16[48,2,256]{2,1,0:T(2,128)(2,1)}, u32[]{:S(2)}, u32[]{:S(2)}) collective-permute-start(bf16[48,2,256]{2,1,0:T(2,128)(2,1)} %reshape.74), channel_id=1, source_target_pairs={{0,15},{1,0},{2,1},{3,2},{4,3},{5,4},{6,5},{7,6},{8,7},{9,8},{10,9... | collective-permute-start | bytes 147464 | tf_op jit(solution)/shard_map/ppermute | solution.py:61
  152.0 6.6 %collective-permute-start.2 = (bf16[48,2,256]{2,1,0:T(2,128)(2,1)}, bf16[48,2,256]{2,1,0:T(2,128)(2,1)}, u32[]{:S(2)}, u32[]{:S(2)}) collective-permute-start(bf16[48,2,256]{2,1,0:T(2,128)(2,1)} %collective-permute-done), channel_id=1, source_target_pairs={{0,1},{1,2},{2,3},{3,4},{4,5},{5,6},{6,7},{7,8},{8,9},{9,10},{10,1... | collective-permute-start | bytes 147464 | tf_op jit(solution)/shard_map/ppermute | solution.py:56
  153.0 6.6 %collective-permute-start.3 = (bf16[48,2,256]{2,1,0:T(2,128)(2,1)}, bf16[48,2,256]{2,1,0:T(2,128)(2,1)}, u32[]{:S(2)}, u32[]{:S(2)}) collective-permute-start(bf16[48,2,256]{2,1,0:T(2,128)(2,1)} %collective-permute-done.1), channel_id=1, source_target_pairs={{0,15},{1,0},{2,1},{3,2},{4,3},{5,4},{6,5},{7,6},{8,7},{9,8},{10,9... | collective-permute-start | bytes 147464 | tf_op jit(solution)/shard_map/ppermute | solution.py:61
  159.5 6.6 %collective-permute-start.4 = (bf16[48,2,256]{2,1,0:T(2,128)(2,1)}, bf16[48,2,256]{2,1,0:T(2,128)(2,1)}, u32[]{:S(2)}, u32[]{:S(2)}) collective-permute-start(bf16[48,2,256]{2,1,0:T(2,128)(2,1)} %collective-permute-done.2), channel_id=1, source_target_pairs={{0,1},{1,2},{2,3},{3,4},{4,5},{5,6},{6,7},{7,8},{8,9},{9,10},{10,1... | collective-permute-start | bytes 147464 | tf_op jit(solution)/shard_map/ppermute | solution.py:56
  160.6 6.6 %collective-permute-start.5 = (bf16[48,2,256]{2,1,0:T(2,128)(2,1)}, bf16[48,2,256]{2,1,0:T(2,128)(2,1)}, u32[]{:S(2)}, u32[]{:S(2)}) collective-permute-start(bf16[48,2,256]{2,1,0:T(2,128)(2,1)} %collective-permute-done.3), channel_id=1, source_target_pairs={{0,15},{1,0},{2,1},{3,2},{4,3},{5,4},{6,5},{7,6},{8,7},{9,8},{10,9... | collective-permute-start | bytes 147464 | tf_op jit(solution)/shard_map/ppermute | solution.py:61
  167.1 6.6 %collective-permute-start.6 = (bf16[48,2,256]{2,1,0:T(2,128)(2,1)}, bf16[48,2,256]{2,1,0:T(2,128)(2,1)}, u32[]{:S(2)}, u32[]{:S(2)}) collective-permute-start(bf16[48,2,256]{2,1,0:T(2,128)(2,1)} %collective-permute-done.4), channel_id=1, source_target_pairs={{0,1},{1,2},{2,3},{3,4},{4,5},{5,6},{6,7},{7,8},{8,9},{9,10},{10,1... | collective-permute-start | bytes 147464 | tf_op jit(solution)/shard_map/ppermute | solution.py:56
  168.1 6.6 %collective-permute-start.7 = (bf16[48,2,256]{2,1,0:T(2,128)(2,1)}, bf16[48,2,256]{2,1,0:T(2,128)(2,1)}, u32[]{:S(2)}, u32[]{:S(2)}) collective-permute-start(bf16[48,2,256]{2,1,0:T(2,128)(2,1)} %collective-permute-done.5), channel_id=1, source_target_pairs={{0,15},{1,0},{2,1},{3,2},{4,3},{5,4},{6,5},{7,6},{8,7},{9,8},{10,9... | collective-permute-start | bytes 147464 | tf_op jit(solution)/shard_map/ppermute | solution.py:61
  174.6 6.6 %collective-permute-start.8 = (bf16[48,2,256]{2,1,0:T(2,128)(2,1)}, bf16[48,2,256]{2,1,0:T(2,128)(2,1)}, u32[]{:S(2)}, u32[]{:S(2)}) collective-permute-start(bf16[48,2,256]{2,1,0:T(2,128)(2,1)} %collective-permute-done.6), channel_id=1, source_target_pairs={{0,1},{1,2},{2,3},{3,4},{4,5},{5,6},{6,7},{7,8},{8,9},{9,10},{10,1... | collective-permute-start | bytes 147464 | tf_op jit(solution)/shard_map/ppermute | solution.py:56
  175.6 6.6 %collective-permute-start.9 = (bf16[48,2,256]{2,1,0:T(2,128)(2,1)}, bf16[48,2,256]{2,1,0:T(2,128)(2,1)}, u32[]{:S(2)}, u32[]{:S(2)}) collective-permute-start(bf16[48,2,256]{2,1,0:T(2,128)(2,1)} %collective-permute-done.7), channel_id=1, source_target_pairs={{0,15},{1,0},{2,1},{3,2},{4,3},{5,4},{6,5},{7,6},{8,7},{9,8},{10,9... | collective-permute-start | bytes 147464 | tf_op jit(solution)/shard_map/ppermute | solution.py:61
  182.1 6.6 %collective-permute-start.10 = (bf16[48,2,256]{2,1,0:T(2,128)(2,1)}, bf16[48,2,256]{2,1,0:T(2,128)(2,1)}, u32[]{:S(2)}, u32[]{:S(2)}) collective-permute-start(bf16[48,2,256]{2,1,0:T(2,128)(2,1)} %collective-permute-done.8), channel_id=1, source_target_pairs={{0,1},{1,2},{2,3},{3,4},{4,5},{5,6},{6,7},{7,8},{8,9},{9,10},{10,1... | collective-permute-start | bytes 147464 | tf_op jit(solution)/shard_map/ppermute | solution.py:56
  183.2 6.6 %collective-permute-start.11 = (bf16[48,2,256]{2,1,0:T(2,128)(2,1)}, bf16[48,2,256]{2,1,0:T(2,128)(2,1)}, u32[]{:S(2)}, u32[]{:S(2)}) collective-permute-start(bf16[48,2,256]{2,1,0:T(2,128)(2,1)} %collective-permute-done.9), channel_id=1, source_target_pairs={{0,15},{1,0},{2,1},{3,2},{4,3},{5,4},{6,5},{7,6},{8,7},{9,8},{10,9... | collective-permute-start | bytes 147464 | tf_op jit(solution)/shard_map/ppermute | solution.py:61
  189.7 6.6 %collective-permute-start.12 = (bf16[48,2,256]{2,1,0:T(2,128)(2,1)}, bf16[48,2,256]{2,1,0:T(2,128)(2,1)}, u32[]{:S(2)}, u32[]{:S(2)}) collective-permute-start(bf16[48,2,256]{2,1,0:T(2,128)(2,1)} %collective-permute-done.10), channel_id=1, source_target_pairs={{0,1},{1,2},{2,3},{3,4},{4,5},{5,6},{6,7},{7,8},{8,9},{9,10},{10,1... | collective-permute-start | bytes 147464 | tf_op jit(solution)/shard_map/ppermute | solution.py:56
  190.7 6.6 %collective-permute-start.13 = (bf16[48,2,256]{2,1,0:T(2,128)(2,1)}, bf16[48,2,256]{2,1,0:T(2,128)(2,1)}, u32[]{:S(2)}, u32[]{:S(2)}) collective-permute-start(bf16[48,2,256]{2,1,0:T(2,128)(2,1)} %collective-permute-done.11), channel_id=1, source_target_pairs={{0,15},{1,0},{2,1},{3,2},{4,3},{5,4},{6,5},{7,6},{8,7},{9,8},{10,9... | collective-permute-start | bytes 147464 | tf_op jit(solution)/shard_map/ppermute | solution.py:61
  197.2 6.6 %collective-permute-start.14 = (bf16[48,2,256]{2,1,0:T(2,128)(2,1)}, bf16[48,2,256]{2,1,0:T(2,128)(2,1)}, u32[]{:S(2)}, u32[]{:S(2)}) collective-permute-start(bf16[48,2,256]{2,1,0:T(2,128)(2,1)} %collective-permute-done.12), channel_id=1, source_target_pairs={{0,1},{1,2},{2,3},{3,4},{4,5},{5,6},{6,7},{7,8},{8,9},{9,10},{10,1... | collective-permute-start | bytes 147464 | tf_op jit(solution)/shard_map/ppermute | solution.py:56
  247.2 14.2 %copy-start.7 = (f32[2,13,256]{2,1,0:T(8,128)S(1)}, f32[2,13,256]{2,1,0:T(8,128)}, u32[]{:S(2)}) copy-start(f32[2,13,256]{2,1,0:T(8,128)} %get-tuple-element.29) | copy-start | bytes 79876
  247.2 14.2 %copy-start.13 = (pred[2,13,256]{2,1,0:T(8,128)(4,1)S(1)}, pred[2,13,256]{2,1,0:T(8,128)(4,1)}, u32[]{:S(2)}) copy-start(pred[2,13,256]{2,1,0:T(8,128)(4,1)} %copy.226) | copy-start | bytes 19972
  247.2 19.7 %copy-start.8 = (f32[2,13,256]{2,1,0:T(8,128)S(1)}, f32[2,13,256]{2,1,0:T(8,128)}, u32[]{:S(2)}) copy-start(f32[2,13,256]{2,1,0:T(8,128)} %get-tuple-element.30) | copy-start | bytes 79876
  247.2 19.7 %copy-start.14 = (pred[2,13,256]{2,1,0:T(8,128)(4,1)S(1)}, pred[2,13,256]{2,1,0:T(8,128)(4,1)}, u32[]{:S(2)}) copy-start(pred[2,13,256]{2,1,0:T(8,128)(4,1)} %copy.220) | copy-start | bytes 19972
  261.4 11.0 %copy-start.4 = (bf16[6656,48]{1,0:T(8,128)(2,1)S(1)}, bf16[6656,48]{1,0:T(8,128)(2,1)}, u32[]{:S(2)}) copy-start(bf16[6656,48]{1,0:T(8,128)(2,1)} %gather_fusion) | copy-start | bytes 1916932
  261.4 11.0 %copy-start.6 = (f32[2,13,256]{2,1,0:T(8,128)S(1)}, f32[2,13,256]{2,1,0:T(8,128)}, u32[]{:S(2)}) copy-start(f32[2,13,256]{2,1,0:T(8,128)} %get-tuple-element.31) | copy-start | bytes 79876
  261.4 11.0 %copy-start.15 = (pred[2,13,256]{2,1,0:T(8,128)(4,1)S(1)}, pred[2,13,256]{2,1,0:T(8,128)(4,1)}, u32[]{:S(2)}) copy-start(pred[2,13,256]{2,1,0:T(8,128)(4,1)} %copy.196) | copy-start | bytes 19972
  266.9 8.0 %copy-start.3 = (bf16[6656,48]{1,0:T(8,128)(2,1)S(1)}, bf16[6656,48]{1,0:T(8,128)(2,1)}, u32[]{:S(2)}) copy-start(bf16[6656,48]{1,0:T(8,128)(2,1)} %gather_fusion.3) | copy-start | bytes 1916932
  266.9 8.0 %copy-start.16 = (pred[2,13,256]{2,1,0:T(8,128)(4,1)S(1)}, pred[2,13,256]{2,1,0:T(8,128)(4,1)}, u32[]{:S(2)}) copy-start(pred[2,13,256]{2,1,0:T(8,128)(4,1)} %copy.232) | copy-start | bytes 19972
  277.9 7.2 %collective-permute-start.15 = (bf16[48,2,256]{0,2,1:T(8,128)(2,1)S(1)}, bf16[48,2,256]{0,2,1:T(8,128)(2,1)S(1)}, u32[]{:S(2)}, u32[]{:S(2)}) collective-permute-start(bf16[48,2,256]{0,2,1:T(8,128)(2,1)S(1)} %get-tuple-element.7), channel_id=1, source_target_pairs={{0,1},{1,2},{2,3},{3,4},{4,5},{5,6},{6,7},{7,8},{8,9},{9,10},{10,1... | collective-permute-start | bytes 147464 | tf_op jit(solution)/shard_map/ppermute | solution.py:56
  277.9 7.2 %collective-permute-start.16 = (bf16[48,2,256]{0,2,1:T(8,128)(2,1)S(1)}, bf16[48,2,256]{0,2,1:T(8,128)(2,1)S(1)}, u32[]{:S(2)}, u32[]{:S(2)}) collective-permute-start(bf16[48,2,256]{0,2,1:T(8,128)(2,1)S(1)} %get-tuple-element.7), channel_id=1, source_target_pairs={{0,15},{1,0},{2,1},{3,2},{4,3},{5,4},{6,5},{7,6},{8,7},{9,8},{10,9... | collective-permute-start | bytes 147464 | tf_op jit(solution)/shard_map/ppermute | solution.py:61
  285.1 7.2 %collective-permute-start.17 = (bf16[48,2,256]{0,2,1:T(8,128)(2,1)S(1)}, bf16[48,2,256]{0,2,1:T(8,128)(2,1)S(1)}, u32[]{:S(2)}, u32[]{:S(2)}) collective-permute-start(bf16[48,2,256]{0,2,1:T(8,128)(2,1)S(1)} %collective-permute-done.15), channel_id=1, source_target_pairs={{0,1},{1,2},{2,3},{3,4},{4,5},{5,6},{6,7},{7,8},{8,9},{9,10},{10,1... | collective-permute-start | bytes 147464 | tf_op jit(solution)/shard_map/ppermute | solution.py:56
  285.1 7.2 %collective-permute-start.18 = (bf16[48,2,256]{0,2,1:T(8,128)(2,1)S(1)}, bf16[48,2,256]{0,2,1:T(8,128)(2,1)S(1)}, u32[]{:S(2)}, u32[]{:S(2)}) collective-permute-start(bf16[48,2,256]{0,2,1:T(8,128)(2,1)S(1)} %collective-permute-done.16), channel_id=1, source_target_pairs={{0,15},{1,0},{2,1},{3,2},{4,3},{5,4},{6,5},{7,6},{8,7},{9,8},{10,9... | collective-permute-start | bytes 147464 | tf_op jit(solution)/shard_map/ppermute | solution.py:61
  292.3 7.2 %collective-permute-start.19 = (bf16[48,2,256]{0,2,1:T(8,128)(2,1)S(1)}, bf16[48,2,256]{0,2,1:T(8,128)(2,1)S(1)}, u32[]{:S(2)}, u32[]{:S(2)}) collective-permute-start(bf16[48,2,256]{0,2,1:T(8,128)(2,1)S(1)} %collective-permute-done.17), channel_id=1, source_target_pairs={{0,1},{1,2},{2,3},{3,4},{4,5},{5,6},{6,7},{7,8},{8,9},{9,10},{10,1... | collective-permute-start | bytes 147464 | tf_op jit(solution)/shard_map/ppermute | solution.py:56
  292.3 7.2 %collective-permute-start.20 = (bf16[48,2,256]{0,2,1:T(8,128)(2,1)S(1)}, bf16[48,2,256]{0,2,1:T(8,128)(2,1)S(1)}, u32[]{:S(2)}, u32[]{:S(2)}) collective-permute-start(bf16[48,2,256]{0,2,1:T(8,128)(2,1)S(1)} %collective-permute-done.18), channel_id=1, source_target_pairs={{0,15},{1,0},{2,1},{3,2},{4,3},{5,4},{6,5},{7,6},{8,7},{9,8},{10,9... | collective-permute-start | bytes 147464 | tf_op jit(solution)/shard_map/ppermute | solution.py:61
  299.5 7.2 %collective-permute-start.21 = (bf16[48,2,256]{0,2,1:T(8,128)(2,1)S(1)}, bf16[48,2,256]{0,2,1:T(8,128)(2,1)S(1)}, u32[]{:S(2)}, u32[]{:S(2)}) collective-permute-start(bf16[48,2,256]{0,2,1:T(8,128)(2,1)S(1)} %collective-permute-done.19), channel_id=1, source_target_pairs={{0,1},{1,2},{2,3},{3,4},{4,5},{5,6},{6,7},{7,8},{8,9},{9,10},{10,1... | collective-permute-start | bytes 147464 | tf_op jit(solution)/shard_map/ppermute | solution.py:56
  299.5 7.2 %collective-permute-start.22 = (bf16[48,2,256]{0,2,1:T(8,128)(2,1)S(1)}, bf16[48,2,256]{0,2,1:T(8,128)(2,1)S(1)}, u32[]{:S(2)}, u32[]{:S(2)}) collective-permute-start(bf16[48,2,256]{0,2,1:T(8,128)(2,1)S(1)} %collective-permute-done.20), channel_id=1, source_target_pairs={{0,15},{1,0},{2,1},{3,2},{4,3},{5,4},{6,5},{7,6},{8,7},{9,8},{10,9... | collective-permute-start | bytes 147464 | tf_op jit(solution)/shard_map/ppermute | solution.py:61
  306.7 7.2 %collective-permute-start.23 = (bf16[48,2,256]{0,2,1:T(8,128)(2,1)S(1)}, bf16[48,2,256]{0,2,1:T(8,128)(2,1)S(1)}, u32[]{:S(2)}, u32[]{:S(2)}) collective-permute-start(bf16[48,2,256]{0,2,1:T(8,128)(2,1)S(1)} %collective-permute-done.21), channel_id=1, source_target_pairs={{0,1},{1,2},{2,3},{3,4},{4,5},{5,6},{6,7},{7,8},{8,9},{9,10},{10,1... | collective-permute-start | bytes 147464 | tf_op jit(solution)/shard_map/ppermute | solution.py:56
  306.7 7.2 %collective-permute-start.24 = (bf16[48,2,256]{0,2,1:T(8,128)(2,1)S(1)}, bf16[48,2,256]{0,2,1:T(8,128)(2,1)S(1)}, u32[]{:S(2)}, u32[]{:S(2)}) collective-permute-start(bf16[48,2,256]{0,2,1:T(8,128)(2,1)S(1)} %collective-permute-done.22), channel_id=1, source_target_pairs={{0,15},{1,0},{2,1},{3,2},{4,3},{5,4},{6,5},{7,6},{8,7},{9,8},{10,9... | collective-permute-start | bytes 147464 | tf_op jit(solution)/shard_map/ppermute | solution.py:61
  313.8 7.2 %collective-permute-start.25 = (bf16[48,2,256]{0,2,1:T(8,128)(2,1)S(1)}, bf16[48,2,256]{0,2,1:T(8,128)(2,1)S(1)}, u32[]{:S(2)}, u32[]{:S(2)}) collective-permute-start(bf16[48,2,256]{0,2,1:T(8,128)(2,1)S(1)} %collective-permute-done.23), channel_id=1, source_target_pairs={{0,1},{1,2},{2,3},{3,4},{4,5},{5,6},{6,7},{7,8},{8,9},{9,10},{10,1... | collective-permute-start | bytes 147464 | tf_op jit(solution)/shard_map/ppermute | solution.py:56
  313.9 7.2 %collective-permute-start.26 = (bf16[48,2,256]{0,2,1:T(8,128)(2,1)S(1)}, bf16[48,2,256]{0,2,1:T(8,128)(2,1)S(1)}, u32[]{:S(2)}, u32[]{:S(2)}) collective-permute-start(bf16[48,2,256]{0,2,1:T(8,128)(2,1)S(1)} %collective-permute-done.24), channel_id=1, source_target_pairs={{0,15},{1,0},{2,1},{3,2},{4,3},{5,4},{6,5},{7,6},{8,7},{9,8},{10,9... | collective-permute-start | bytes 147464 | tf_op jit(solution)/shard_map/ppermute | solution.py:61
  321.0 7.1 %collective-permute-start.27 = (bf16[48,2,256]{0,2,1:T(8,128)(2,1)S(1)}, bf16[48,2,256]{0,2,1:T(8,128)(2,1)S(1)}, u32[]{:S(2)}, u32[]{:S(2)}) collective-permute-start(bf16[48,2,256]{0,2,1:T(8,128)(2,1)S(1)} %collective-permute-done.25), channel_id=1, source_target_pairs={{0,1},{1,2},{2,3},{3,4},{4,5},{5,6},{6,7},{7,8},{8,9},{9,10},{10,1... | collective-permute-start | bytes 147464 | tf_op jit(solution)/shard_map/ppermute | solution.py:56
  321.1 7.1 %collective-permute-start.28 = (bf16[48,2,256]{0,2,1:T(8,128)(2,1)S(1)}, bf16[48,2,256]{0,2,1:T(8,128)(2,1)S(1)}, u32[]{:S(2)}, u32[]{:S(2)}) collective-permute-start(bf16[48,2,256]{0,2,1:T(8,128)(2,1)S(1)} %collective-permute-done.26), channel_id=1, source_target_pairs={{0,15},{1,0},{2,1},{3,2},{4,3},{5,4},{6,5},{7,6},{8,7},{9,8},{10,9... | collective-permute-start | bytes 147464 | tf_op jit(solution)/shard_map/ppermute | solution.py:61
  328.1 7.1 %collective-permute-start.29 = (bf16[48,2,256]{0,2,1:T(8,128)(2,1)S(1)}, bf16[48,2,256]{0,2,1:T(8,128)(2,1)S(1)}, u32[]{:S(2)}, u32[]{:S(2)}) collective-permute-start(bf16[48,2,256]{0,2,1:T(8,128)(2,1)S(1)} %collective-permute-done.27), channel_id=1, source_target_pairs={{0,1},{1,2},{2,3},{3,4},{4,5},{5,6},{6,7},{7,8},{8,9},{9,10},{10,1... | collective-permute-start | bytes 147464 | tf_op jit(solution)/shard_map/ppermute | solution.py:56
  391.8 11.0 %copy-start.2 = (bf16[6656,48]{1,0:T(8,128)(2,1)S(1)}, bf16[6656,48]{1,0:T(8,128)(2,1)}, u32[]{:S(2)}) copy-start(bf16[6656,48]{1,0:T(8,128)(2,1)} %gather_fusion.4) | copy-start | bytes 1916932
  397.3 7.9 %copy-start.1 = (bf16[6656,48]{1,0:T(8,128)(2,1)S(1)}, bf16[6656,48]{1,0:T(8,128)(2,1)}, u32[]{:S(2)}) copy-start(bf16[6656,48]{1,0:T(8,128)(2,1)} %gather_fusion.7) | copy-start | bytes 1916932
  405.2 2.6 copy-start.11
  (2 other events, 3.7 us)
Sparse Core Ops, SparseCore 0:
  12.9 127.3 all-reduce.1
